TPU v7x, 32 devices: a whole 2x2x4 slice. The times are simulated.
32 devices in a mesh: parts: 2 (over y), row: 4 (over z), col: 4 (over x, core), sub: 1.
Axes of the slice: x: 2, y: 2, z: 4, core: 2. Of those that a mesh axis runs over, the one named last changes fastest.
Arguments:
- activations: bfloat16 [1024, 2048], P(('parts', 'row'), ('col', 'sub')), parts along dimension 0, may hold values from -6 to 6
- expert_ids: int32 [1024, 8], P(('parts', 'row')), parts along dimension 0, may hold values from 0 to 15, all different within a row; in each aligned block of 32 rows (0 to 31, 32 to 63, ...) at most 32 rows name the same one
- gate_scores: float32 [1024, 8], P(('parts', 'row')), parts along dimension 0, may hold values from 0.05 to 0.5
- gate_proj: bfloat16 [16, 2048, 768], P(('row', 'col'), None, 'sub'), may hold values from -0.125 to 0.125
- up_proj: bfloat16 [16, 2048, 768], P(('row', 'col'), None, 'sub'), may hold values from -0.125 to 0.125
- down_proj: bfloat16 [16, 768, 2048], P(('row', 'col'), 'sub'), may hold values from -0.21875 to 0.21875
Outputs:
- moe_output: bfloat16 [1024, 2048], P(('parts', 'row'), ('col', 'sub')), parts along dimension 0
There are 2 independent parts, one for each index of `parts`. A program takes and returns all parts, laid end to end along the dimension named above; an argument that names none is the same for every part. Nothing has to cross between parts.
Inputs may be any that keep to these rules, and one draw needn't show every extreme that they name: `expert_ids`: each row names 8 different experts. In each aligned block of 32 rows no expert is named by more than 32 rows, a bound that some block reaches.
All inputs are finite; a program needn't handle non-finite values.
Results may differ from a plain program's by a relative error of at most 0.0057.
Values may be sent and summed in bfloat16 or wider, within the bound.
No kernel may reach another device: no remote copies, remote signals or barrier semaphores. Data moves between devices by JAX's collectives and lax.ppermute only.
A program may use at most 64 MiB of HBM per device.

v0:
```python
import jax
import jax.numpy as jnp
from jax import lax
from jax.sharding import PartitionSpec as P

TOP = 8


def slot_places(chosen, experts, capacity):
    count = chosen.shape[0] * chosen.shape[1]
    flat_ids = chosen.reshape(count)
    onehot = (flat_ids[:, None] == jnp.arange(experts, dtype=jnp.int32)[None, :]).astype(jnp.int32)
    running = jnp.cumsum(onehot, axis=0) - 1
    ranking = jnp.sum(onehot * running, axis=1)
    return flat_ids * capacity + ranking


def fill_slots(row_block, places, experts, capacity, top_count):
    owners = jnp.full((experts * capacity,), row_block.shape[0], jnp.int32)
    owners = owners.at[places].set(jnp.arange(places.shape[0], dtype=jnp.int32) // top_count)
    padded = jnp.concatenate(
        [row_block, jnp.zeros((1, row_block.shape[1]), row_block.dtype)], axis=0
    )
    return padded[owners].reshape(experts, capacity, row_block.shape[1])


def run_expert(stacked, gate_proj, up_proj, down_proj):
    layout = stacked.shape
    inputs = stacked.reshape(-1, layout[-1])
    gate_val = jnp.dot(inputs, gate_proj[0], preferred_element_type=jnp.float32)
    up_val = jnp.dot(inputs, up_proj[0], preferred_element_type=jnp.float32)
    hidden = (jax.nn.silu(gate_val) * up_val).astype(jnp.bfloat16)
    partial_out = jnp.dot(hidden, down_proj[0], preferred_element_type=jnp.float32)
    return partial_out.reshape(layout)


def send_back(stacked, gate_proj, up_proj, down_proj):
    partial_out = run_expert(stacked, gate_proj, up_proj, down_proj)
    landed = lax.all_to_all(partial_out, ("row", "col"), split_axis=1, concat_axis=1, tiled=True)
    return lax.psum_scatter(landed, "sub", scatter_dimension=0, tiled=True).astype(jnp.bfloat16)


def per_device(activations, expert_ids, gate_scores, gate_proj, up_proj, down_proj):
    col_count = lax.axis_size("col")
    sub_count = lax.axis_size("sub")
    experts = lax.axis_size("row") * col_count
    group_rows = expert_ids.shape[0]
    block_rows = group_rows // (col_count * sub_count)
    capacity = max(2, min(block_rows, 2 * block_rows * TOP // experts))
    quarter = sub_count * block_rows
    width = activations.shape[1] * col_count * sub_count
    whole = lax.all_gather(activations, ("col", "sub"), axis=1, tiled=True)
    col_start = lax.axis_index("col") * quarter
    sub_index = lax.axis_index("sub")
    my_rows = lax.dynamic_slice_in_dim(whole, col_start, quarter, 0)
    my_ids = lax.dynamic_slice_in_dim(expert_ids, col_start, quarter, 0)
    own_scores = lax.dynamic_slice_in_dim(
        gate_scores, col_start + sub_index * block_rows, block_rows, 0
    )
    places = []
    for member in range(sub_count):
        lower = member * block_rows
        places.append(slot_places(my_ids[lower : lower + block_rows], experts, capacity))
    own_places = lax.dynamic_index_in_dim(jnp.stack(places), sub_index, 0, keepdims=False)
    buffers = []
    for member in range(sub_count):
        lower = member * block_rows
        buffers.append(
            fill_slots(my_rows[lower : lower + block_rows], places[member], experts, capacity, TOP)
        )
    outgoing = jnp.stack(buffers)
    returned = send_back(
        lax.all_to_all(outgoing, ("row", "col"), split_axis=1, concat_axis=1, tiled=True),
        gate_proj,
        up_proj,
        down_proj,
    )
    picked = returned.reshape(-1, width)[own_places].reshape(block_rows, TOP, width)
    share = jnp.sum(own_scores[:, :, None] * picked.astype(jnp.float32), axis=1)
    return lax.all_to_all(
        share.astype(jnp.bfloat16), ("col", "sub"), split_axis=1, concat_axis=0, tiled=True
    )


def solution(mesh):
    placed = (
        P(("parts", "row"), ("col", "sub")),
        P(("parts", "row"), None),
        P(("parts", "row"), None),
        P(("row", "col"), None, "sub"),
        P(("row", "col"), None, "sub"),
        P(("row", "col"), "sub", None),
    )
    return jax.shard_map(
        per_device,
        mesh=mesh,
        in_specs=placed,
        out_specs=P(("parts", "row"), ("col", "sub")),
        check_vma=False,
    )
```

profile of v0, /device:TPU:20, one launch (start us, length us, event | category | flops | bytes accessed | tf_op | source)
XLA Modules:
  0.0 142.7 jit_solution(10261888234593727119)
XLA Ops:
  0.0 0.0 copy-start
  0.0 0.9 broadcast_multiply_fusion
  0.9 0.1 copy.21
  1.0 0.1 eq.29
  1.1 0.1 eq.25
  1.2 0.6 reduce-window.6
  1.8 0.2 slice_reduce_fusion
  2.0 0.1 copy.20
  2.1 0.1 mul.43
  2.2 0.1 fusion.9
  2.3 1.4 scatter_custom_fusion
  3.7 7.4 %all_gather.3 = bf16[128,2048]{1,0:T(8,128)(2,1)S(1)} all-gather(bf16[128,512]{1,0:T(8,128)(2,1)} %param.6), channel_id=1, replica_groups=mesh['parts'=2,'row'=4,'col'=4,'sub'=1] {'col','sub'}, dimensions={1}, use_global_device_ids=true | all-gather | bytes 655360 | tf_op jit(solution)/shard_map/all_gather | solution.py:52
  11.1 3.3 %gather_fusion = bf16[512,2048]{1,0:T(8,128)(2,1)} fusion(bf16[33,2048]{1,0:T(8,128)(2,1)S(1)} %concatenate.3, s32[1024]{0:T(1024)S(1)} %pad_clamp_fusion.1), kind=kCustom, calls=%fused_computation | custom fusion | bytes 4196352 | tf_op jit(solution)/shard_map/gather | solution.py:24
  14.5 0.0 copy-start.2
  14.5 53.6 %all_to_all.26 = bf16[1,16,32,2048]{3,2,0,1:T(8,128)(2,1)S(1)} all-to-all(bf16[1,16,32,2048]{3,2,0,1:T(8,128)(2,1)} %bitcast.52), channel_id=1, replica_groups=mesh['parts'=2,'row'=4,'col'=4,'sub'=1] {'row','col'}, dimensions={1} | all-to-all | bytes 4194304 | tf_op jit(solution)/shard_map/all_to_all | solution.py:73
  68.1 0.0 copy-done.2
  68.1 0.0 copy-start.3
  68.1 1.8 %fusion.3 = f32[512,768]{1,0:T(8,128)S(1)} fusion(bf16[512,2048]{1,0:T(8,128)(2,1)S(1)} %bitcast.53, bf16[1,2048,768]{2,1,0:T(8,128)(2,1)S(1)} %copy-done.2), kind=kOutput, calls=%fused_computation.7 | convolution fusion | flops 1610612736 | bytes 6815744 | tf_op jit(solution)/shard_map/dot_general | solution.py:30
  69.9 0.1 copy-done.3
  69.9 1.9 %multiply_convert_fusion = bf16[512,768]{1,0:T(8,128)(2,1)S(1)} fusion(f32[512,768]{1,0:T(8,128)S(1)} %fusion.3, bf16[512,2048]{1,0:T(8,128)(2,1)S(1)} %bitcast.54, bf16[1,2048,768]{2,1,0:T(8,128)(2,1)S(1)} %copy-done.3), kind=kOutput, calls=%fused_computation.11 | convolution fusion | flops 1612972032 | bytes 7602176 | tf_op jit(solution)/shard_map/dot_general | solution.py:31
  71.9 0.0 copy-done
  71.9 3.1 %convolution_bitcast_fusion = bf16[1,16,32,2048]{3,2,0,1:T(8,128)(2,1)} fusion(bf16[16,32,768]{2,1,0:T(8,128)(2,1)S(1)} %bitcast.61, bf16[1,768,2048]{2,1,0:T(8,128)(2,1)S(1)} %copy-done), kind=kOutput, calls=%fused_computation.3 | convolution fusion | flops 1610612736 | bytes 6029312 | tf_op jit(solution)/shard_map/dot_general | solution.py:33
  75.0 0.0 copy-start.1
  75.0 4.9 %all-to-all-start.1 = ((bf16[1,16,32,2048]{3,2,0,1:T(8,128)(2,1)}), bf16[1,16,32,2048]{3,2,0,1:T(8,128)(2,1)}, u32[]{:S(2)}, u32[]{:S(2)}) async-start(bf16[1,16,32,2048]{3,2,0,1:T(8,128)(2,1)} %convolution_bitcast_fusion), calls=%async_computation.1 | async-start | bytes 4194304 | tf_op jit(solution)/shard_map/all_to_all | solution.py:39
  79.9 0.0 copy-done.1
  79.9 0.1 constant_dynamic-slice_fusion.2
  80.0 0.1 copy.19
  80.0 47.6 %all-to-all-done.1 = bf16[1,16,32,2048]{3,2,0,1:T(8,128)(2,1)} async-done(((bf16[1,16,32,2048]{3,2,0,1:T(8,128)(2,1)}), bf16[1,16,32,2048]{3,2,0,1:T(8,128)(2,1)}, u32[]{:S(2)}, u32[]{:S(2)}) %all-to-all-start.1) | async-done | bytes 2097184 | tf_op jit(solution)/shard_map/all_to_all | solution.py:39
  127.6 5.2 %gather_fusion.1 = bf16[256,2048]{1,0:T(8,128)(2,1)} fusion(bf16[512,2048]{1,0:T(8,128)(2,1)} %bitcast.13, s32[1024]{0:T(1024)S(1)} %pad_clamp_fusion), kind=kCustom, calls=%fused_computation.1 | custom fusion | bytes 2098176 | tf_op jit(solution)/shard_map/gather | solution.py:78
  132.8 2.2 %fusion.5 = bf16[32,2048]{1,0:T(8,128)(2,1)S(1)} fusion(bf16[256,2048]{1,0:T(8,128)(2,1)} %gather_fusion.1, f32[32,8]{1,0:T(8,128)S(1)} %copy.19), kind=kLoop, calls=%fused_computation.10 | loop fusion | flops 1507328 | bytes 1180672 | tf_op jit(solution)/shard_map/reduce_sum | solution.py:79
  135.0 7.0 %all_to_all.27 = bf16[32,4,512]{2,0,1:T(8,128)(2,1)S(1)} all-to-all(bf16[32,4,512]{2,0,1:T(8,128)(2,1)S(1)} %bitcast.56), channel_id=1, replica_groups=mesh['parts'=2,'row'=4,'col'=4,'sub'=1] {'col','sub'}, dimensions={1} | all-to-all | bytes 262144 | tf_op jit(solution)/shard_map/all_to_all | solution.py:80
  142.0 0.7 copy.33
  (11 shorter events, 0.1 us)
Async XLA Ops:
  0.0 71.9 %copy-start = (bf16[1,768,2048]{2,1,0:T(8,128)(2,1)S(1)}, bf16[1,768,2048]{2,1,0:T(8,128)(2,1)}, u32[]{:S(2)}) copy-start(bf16[1,768,2048]{2,1,0:T(8,128)(2,1)} %param.11) | copy-start | bytes 9437188
  14.5 53.6 %copy-start.2 = (bf16[1,2048,768]{2,1,0:T(8,128)(2,1)S(1)}, bf16[1,2048,768]{2,1,0:T(8,128)(2,1)}, u32[]{:S(2)}) copy-start(bf16[1,2048,768]{2,1,0:T(8,128)(2,1)} %param.9) | copy-start | bytes 9437188
  68.1 1.9 %copy-start.3 = (bf16[1,2048,768]{2,1,0:T(8,128)(2,1)S(1)}, bf16[1,2048,768]{2,1,0:T(8,128)(2,1)}, u32[]{:S(2)}) copy-start(bf16[1,2048,768]{2,1,0:T(8,128)(2,1)} %param.10) | copy-start | bytes 9437188
  75.0 4.9 %copy-start.1 = (f32[128,8]{0,1:T(8,128)S(1)}, f32[128,8]{0,1:T(8,128)}, u32[]{:S(2)}) copy-start(f32[128,8]{0,1:T(8,128)} %param.8) | copy-start | bytes 12292
  75.0 52.6 %all-to-all-start.1 = ((bf16[1,16,32,2048]{3,2,0,1:T(8,128)(2,1)}), bf16[1,16,32,2048]{3,2,0,1:T(8,128)(2,1)}, u32[]{:S(2)}, u32[]{:S(2)}) async-start(bf16[1,16,32,2048]{3,2,0,1:T(8,128)(2,1)} %convolution_bitcast_fusion), calls=%async_computation.1 | async-start | bytes 4194304 | tf_op jit(solution)/shard_map/all_to_all | solution.py:39
where the time goes:
time: 143 us
  blocking collectives  67.9 us (47%)
  waiting for transfers between devices  47.6 us (33%)
  local copies, waits for them, and re-layouts  11.5 us (8%)
  matrix products  6.85 us (5%)
  starting transfers between devices  4.86 us (3%)
  other arithmetic  3.86 us (3%)
    all_to_all x1, blocking collectives, per_device(): lax.all_to_all(outgoing, ('row', 'col'), split_axis=1, concat_axis=1, til...  53.6 us
    all_to_all x1, waiting for transfers between devices, send_back(): lax.all_to_all(partial_out, ('row', 'col'), split_axis=1, concat_axis=1,...  47.6 us
    all_gather x1, blocking collectives, per_device(): whole = lax.all_gather(activations, ('col', 'sub'), axis=1, tiled=True)  7.38 us
    all_to_all x1, blocking collectives, per_device(): lax.all_to_all(share.astype(jnp.bfloat16), ('col', 'sub'), split_axis=1,...  6.99 us
    gather x1, local copies, waits for them, and re-layouts, per_device(): returned.reshape(-1, width)[own_places].reshape(block_rows, TOP, width)  5.21 us
    all_to_all x1, starting transfers between devices, send_back(): lax.all_to_all(partial_out, ('row', 'col'), split_axis=1, concat_axis=1,...  4.86 us
    gather x1, local copies, waits for them, and re-layouts, fill_slots(): return padded[owners].reshape(experts, capacity, row_block.shape[1])  3.35 us
    dot_general x1, matrix products, run_expert(): jnp.dot(hidden, down_proj[0], preferred_element_type=jnp.float32)  3.14 us
  transfers between devices with their start and end apart: 1, of which 1 were waited for; matrix products, arithmetic and copies ran while one was open for 0% of the time, Pallas kernels for 0%

commit v1 on v0

--- a/solution.py
+++ b/solution.py
@@ -1,6 +1,11 @@
+import functools
+import math
+
 import jax
 import jax.numpy as jnp
 from jax import lax
+from jax.experimental import pallas as pl
+from jax.experimental.pallas import tpu as pltpu
 from jax.sharding import PartitionSpec as P
 
 TOP = 8
@@ -40,7 +45,7 @@
     return lax.psum_scatter(landed, "sub", scatter_dimension=0, tiled=True).astype(jnp.bfloat16)
 
 
-def per_device(activations, expert_ids, gate_scores, gate_proj, up_proj, down_proj):
+def routed(activations, expert_ids, gate_scores, gate_proj, up_proj, down_proj):
     col_count = lax.axis_size("col")
     sub_count = lax.axis_size("sub")
     experts = lax.axis_size("row") * col_count
@@ -82,6 +87,168 @@
     )
 
 
+def swap(value, axis, bit):
+    count = lax.axis_size(axis)
+    return lax.ppermute(value, axis, [(i, i ^ bit) for i in range(count)])
+
+
+def expert_kernel(group, feats, place, *refs):
+    blocks = len(group)
+    tables, refs = refs[:blocks], refs[blocks:]
+    xs, refs = refs[: blocks * feats], refs[blocks * feats :]
+    gate, up, down, kept, sent, whole, hidden = refs
+    col, expert = place[0], place[1].astype(jnp.float32)
+    rows, depth = xs[0].shape
+    units = gate.shape[1]
+    tile = math.gcd(units, 256)
+    for m in range(feats):
+        start = pl.multiple_of((col ^ m) * depth, depth)
+        for j in range(blocks):
+            whole[j * rows : (j + 1) * rows, pl.ds(start, depth)] = xs[j * feats + m][...]
+    for h in range(0, units, tile):
+        g = jnp.dot(whole[...], gate[:, h : h + tile], preferred_element_type=jnp.float32)
+        u = jnp.dot(whole[...], up[:, h : h + tile], preferred_element_type=jnp.float32)
+        hidden[:, h : h + tile] = (g / (1.0 + jnp.exp(-g)) * u).astype(jnp.bfloat16)
+    wide = []
+    for j in range(blocks):
+        ids, scores = tables[j][:TOP], tables[j][TOP:]
+        weight = jnp.sum(jnp.where(ids == expert, scores, 0.0), axis=0, keepdims=True)
+        wide.append(jnp.broadcast_to(weight, (128, rows)).T)
+    wide = jnp.concatenate(wide, axis=0)
+    wide = jnp.concatenate([wide] * (tile // 128), axis=1)
+    for m in [*range(1, feats, 2), *range(0, feats, 2)]:
+        target = sent if m & 1 else kept
+        for n in range(0, depth, tile):
+            start = pl.multiple_of((col ^ m) * depth + n, tile)
+            y = jnp.dot(hidden[...], down[:, pl.ds(start, tile)], preferred_element_type=jnp.float32)
+            place_in = m // 2 * depth + n
+            target[:, place_in : place_in + tile] = (y * wide).astype(target.dtype)
+
+
+def full_specs(count):
+    return [pl.BlockSpec(memory_space=pltpu.VMEM)] * count
+
+
+def run_expert_group(place, group, tables, xs, gate, up, down, feats):
+    blocks = len(group)
+    rows, depth = xs[0].shape
+    units = gate.shape[1]
+    out = (blocks * rows, feats // 2 * depth)
+    return pl.pallas_call(
+        functools.partial(expert_kernel, group, feats),
+        out_shape=[jax.ShapeDtypeStruct(out, jnp.float32), jax.ShapeDtypeStruct(out, jnp.bfloat16)],
+        in_specs=[pl.BlockSpec(memory_space=pltpu.SMEM)] + full_specs(blocks + 3 + len(xs)),
+        out_specs=full_specs(2),
+        scratch_shapes=[
+            pltpu.VMEM((blocks * rows, feats * depth), jnp.bfloat16),
+            pltpu.VMEM((blocks * rows, units), jnp.bfloat16),
+        ],
+        cost_estimate=pl.CostEstimate(
+            flops=6 * blocks * rows * depth * feats * units, bytes_accessed=1 << 20, transcendentals=0
+        ),
+        compiler_params=pltpu.CompilerParams(vmem_limit_bytes=16 << 20),
+        name="expert",
+    )(place, *tables, *xs, gate, up, down)
+
+
+def join_kernel(blocks, feats, kept, got, *outs):
+    rows = outs[0].shape[0]
+    depth = outs[0].shape[1]
+    for j in range(blocks):
+        for m in range(feats):
+            at = (slice(j * rows, (j + 1) * rows), slice(m * depth, (m + 1) * depth))
+            out = outs[j * feats + m]
+            out[...] = (kept[at] + got[at].astype(jnp.float32)).astype(out.dtype)
+
+
+def run_join(kept, got, blocks, feats):
+    rows, depth = kept.shape[0] // blocks, kept.shape[1] // feats
+    shapes = []
+    for _ in range(blocks):
+        for m in range(feats):
+            shapes.append(jax.ShapeDtypeStruct((rows, depth), jnp.bfloat16 if m else jnp.float32))
+    return pl.pallas_call(
+        functools.partial(join_kernel, blocks, feats),
+        out_shape=shapes,
+        in_specs=full_specs(2),
+        out_specs=full_specs(len(shapes)),
+        cost_estimate=pl.CostEstimate(flops=kept.size, bytes_accessed=kept.size, transcendentals=0),
+        compiler_params=pltpu.CompilerParams(vmem_limit_bytes=8 << 20),
+        name="join",
+    )(kept, got)
+
+
+def sum_kernel(*refs):
+    total = refs[0][...].astype(jnp.float32)
+    for ref in refs[1:-1]:
+        total += ref[...].astype(jnp.float32)
+    refs[-1][...] = total.astype(refs[-1].dtype)
+
+
+def run_sum(values, dtype):
+    return pl.pallas_call(
+        sum_kernel,
+        out_shape=jax.ShapeDtypeStruct(values[0].shape, dtype),
+        in_specs=full_specs(len(values)),
+        out_specs=full_specs(1)[0],
+        cost_estimate=pl.CostEstimate(
+            flops=values[0].size * len(values), bytes_accessed=values[0].size, transcendentals=0
+        ),
+        compiler_params=pltpu.CompilerParams(vmem_limit_bytes=8 << 20),
+        name="total",
+    )(*values)
+
+
+def dense(activations, expert_ids, gate_scores, gate_proj, up_proj, down_proj):
+    row_count, col_count = lax.axis_size("row"), lax.axis_size("col")
+    row, col = lax.axis_index("row"), lax.axis_index("col")
+    place = jnp.stack([col, row * col_count + col]).astype(jnp.int32)
+    packed = jnp.concatenate([expert_ids.astype(jnp.float32).T, gate_scores.T], axis=0)
+    groups = [(0, 2), (1, 3)]
+    far = col_count // 2
+    order = [2, 1, 3]
+    held = {(0, 0): activations}
+    table = {0: packed}
+    for j in order:
+        held[j, 0] = swap(activations, "row", j)
+    held[0, far] = swap(activations, "col", far)
+    for j in order:
+        table[j] = swap(packed, "row", j)
+    results = []
+    for group in groups:
+        for j in group:
+            if j:
+                held[j, far] = swap(held[j, 0], "col", far)
+        for m in (0, far):
+            for j in group:
+                held[j, m ^ 1] = swap(held[j, m], "col", 1)
+    kept, sent, other = {}, {}, {}
+    for group in groups:
+        xs = [held[j, m] for j in group for m in range(col_count)]
+        kept[group], sent[group] = run_expert_group(
+            place, group, [table[j] for j in group], xs, gate_proj[0], up_proj[0], down_proj[0], col_count
+        )
+    total = {}
+    for group in groups:
+        got = swap(sent[group], "col", 1)
+        joined = run_join(kept[group], got, len(group), 2)
+        for i, j in enumerate(group):
+            total[j] = (joined[2 * i], swap(joined[2 * i + 1], "col", far))
+    for j in order:
+        total[j] = (swap(run_sum(total[j], jnp.bfloat16), "row", j),)
+    return run_sum([*total[0], *total[1], *total[2], *total[3]], jnp.bfloat16)
+
+
+def per_device(activations, expert_ids, gate_scores, gate_proj, up_proj, down_proj):
+    row_count, col_count, sub_count = lax.axis_size("row"), lax.axis_size("col"), lax.axis_size("sub")
+    block_rows = expert_ids.shape[0] // (col_count * sub_count)
+    every_row = block_rows * row_count * col_count <= 2 * block_rows * TOP * 1
+    whole = sub_count == 1 and col_count > 1
+    squares = row_count & (row_count - 1) == 0 and col_count & (col_count - 1) == 0
+    chosen = dense if every_row and whole and squares else routed
+    return chosen(activations, expert_ids, gate_scores, gate_proj, up_proj, down_proj)
+
+
 def solution(mesh):
     placed = (
         P(("parts", "row"), ("col", "sub")),

time: 143 us -> 67.1 us (0.47)
  the two profiles are of different devices: /device:TPU:20 before, /device:TPU:0 now
where the time goes in v1:
time: 67.1 us; the launch traced here: 66.8 us
  starting transfers between devices  29.1 us (43%)
  waiting for transfers between devices  23 us (34%)
  Pallas kernels  7.57 us (11%)
  local copies, waits for them, and re-layouts  5.67 us (8%)
  other arithmetic  1.45 us (2%)
    ppermute x27, starting transfers between devices, swap(): return lax.ppermute(value, axis, [(i, i ^ bit) for i in range(count)])  29.1 us
    ppermute x27, waiting for transfers between devices, swap(): return lax.ppermute(value, axis, [(i, i ^ bit) for i in range(count)])  23 us
    pallas_call x2, Pallas kernels, run_expert_group(): pl.pallas_call(functools.partial(expert_kernel, group, feats), out_shape=...  6.56 us
    unnamed x10, local copies, waits for them, and re-layouts  5.67 us
  transfers between devices with their start and end apart: 27, of which 10 were waited for; matrix products, arithmetic and copies ran while one was open for 2% of the time, Pallas kernels for 10%

profile of v1, /device:TPU:0, one launch (start us, length us, event | category | flops | bytes accessed | tf_op | source)
XLA Modules:
  0.0 66.8 jit_solution(1198245762283476916)
XLA Ops:
  0.0 3.1 %collective-permute-start.12 = (bf16[128,512]{1,0:T(8,128)(2,1)}, bf16[128,512]{1,0:T(8,128)(2,1)S(1)}, u32[]{:S(2)}, u32[]{:S(2)}) collective-permute-start(bf16[128,512]{1,0:T(8,128)(2,1)} %refs_2_.1), channel_id=1, source_target_pairs={{0,4},{4,0},{8,12},{12,8},{1,5},{5,1},{9,13},{13,9},{2,6},{6,2},{1... | collective-permute-start | bytes 393224 | tf_op jit(solution)/shard_map/ppermute | solution.py:92
  3.1 2.5 %collective-permute-start.16 = (bf16[128,512]{1,0:T(8,128)(2,1)}, bf16[128,512]{1,0:T(8,128)(2,1)S(1)}, u32[]{:S(2)}, u32[]{:S(2)}) collective-permute-start(bf16[128,512]{1,0:T(8,128)(2,1)} %refs_2_.1), channel_id=1, source_target_pairs={{0,12},{4,8},{8,4},{12,0},{1,13},{5,9},{9,5},{13,1},{2,14},{6,10},... | collective-permute-start | bytes 393224 | tf_op jit(solution)/shard_map/ppermute | solution.py:92
  5.6 1.5 %collective-permute-start.2 = (bf16[128,512]{1,0:T(8,128)(2,1)}, bf16[128,512]{1,0:T(8,128)(2,1)S(1)}, u32[]{:S(2)}, u32[]{:S(2)}) collective-permute-start(bf16[128,512]{1,0:T(8,128)(2,1)} %refs_2_.1), channel_id=1, source_target_pairs={{0,2},{1,3},{2,0},{3,1},{4,6},{5,7},{6,4},{7,5},{8,10},{9,11},{10,... | collective-permute-start | bytes 393224 | tf_op jit(solution)/shard_map/ppermute | solution.py:92
  7.1 1.3 %collective-permute-start.14 = (bf16[128,512]{1,0:T(8,128)(2,1)S(1)}, bf16[128,512]{1,0:T(8,128)(2,1)S(1)}, u32[]{:S(2)}, u32[]{:S(2)}) collective-permute-start(bf16[128,512]{1,0:T(8,128)(2,1)S(1)} %collective-permute-done.12.refs_2_), channel_id=1, source_target_pairs={{0,2},{1,3},{2,0},{3,1},{4,6},{5,7},{6,4},{7,5},{8,10},{9,11},{10,... | collective-permute-start | bytes 393224 | tf_op jit(solution)/shard_map/ppermute | solution.py:92
  8.4 4.6 %collective-permute-done.16.refs_6_ = bf16[128,512]{1,0:T(8,128)(2,1)S(1)} collective-permute-done((bf16[128,512]{1,0:T(8,128)(2,1)}, bf16[128,512]{1,0:T(8,128)(2,1)S(1)}, u32[]{:S(2)}, u32[]{:S(2)}) %collective-permute-start.16) | collective-permute-done | bytes 131104 | tf_op jit(solution)/shard_map/ppermute | solution.py:92
  13.0 1.5 %collective-permute-start.18 = (bf16[128,512]{1,0:T(8,128)(2,1)S(1)}, bf16[128,512]{1,0:T(8,128)(2,1)S(1)}, u32[]{:S(2)}, u32[]{:S(2)}) collective-permute-start(bf16[128,512]{1,0:T(8,128)(2,1)S(1)} %collective-permute-done.16.refs_6_), channel_id=1, source_target_pairs={{0,2},{1,3},{2,0},{3,1},{4,6},{5,7},{6,4},{7,5},{8,10},{9,11},{10,... | collective-permute-start | bytes 393224 | tf_op jit(solution)/shard_map/ppermute | solution.py:92
  14.5 0.7 %convert_bitcast_fusion = f32[8,128]{1,0:T(8,128)S(1)} fusion(s32[128,8]{0,1:T(8,128)} %param.7), kind=kLoop, calls=%fused_computation.1 | loop fusion | flops 1024 | bytes 8192 | tf_op jit(solution)/shard_map/transpose | solution.py:206
  15.2 0.7 %pad_maximum_fusion.refs_0_ = f32[16,128]{1,0:T(8,128)S(1)} fusion(f32[8,128]{1,0:T(8,128)} %bitcast.14, f32[8,128]{1,0:T(8,128)S(1)} %convert_bitcast_fusion), kind=kLoop, calls=%fused_computation | loop fusion | flops 2048 | bytes 16384 | tf_op jit(solution)/shard_map/concatenate | solution.py:206
  15.9 3.2 %collective-permute-start.10 = (f32[16,128]{1,0:T(8,128)S(1)}, f32[16,128]{1,0:T(8,128)S(1)}, u32[]{:S(2)}, u32[]{:S(2)}) collective-permute-start(f32[16,128]{1,0:T(8,128)S(1)} %pad_maximum_fusion.refs_0_), channel_id=1, source_target_pairs={{0,4},{4,0},{8,12},{12,8},{1,5},{5,1},{9,13},{13,9},{2,6},{6,2},{1... | collective-permute-start | bytes 24584 | tf_op jit(solution)/shard_map/ppermute | solution.py:92
  19.1 1.6 %collective-permute-done.10.refs_0_ = f32[16,128]{1,0:T(8,128)S(1)} collective-permute-done((f32[16,128]{1,0:T(8,128)S(1)}, f32[16,128]{1,0:T(8,128)S(1)}, u32[]{:S(2)}, u32[]{:S(2)}) %collective-permute-start.10) | collective-permute-done | bytes 8224 | tf_op jit(solution)/shard_map/ppermute | solution.py:92
  20.7 2.8 %collective-permute-start.11 = (f32[16,128]{1,0:T(8,128)S(1)}, f32[16,128]{1,0:T(8,128)S(1)}, u32[]{:S(2)}, u32[]{:S(2)}) collective-permute-start(f32[16,128]{1,0:T(8,128)S(1)} %pad_maximum_fusion.refs_0_), channel_id=1, source_target_pairs={{0,12},{4,8},{8,4},{12,0},{1,13},{5,9},{9,5},{13,1},{2,14},{6,10},... | collective-permute-start | bytes 24584 | tf_op jit(solution)/shard_map/ppermute | solution.py:92
  23.5 2.7 %collective-permute-done.11.refs_1_ = f32[16,128]{1,0:T(8,128)S(1)} collective-permute-done((f32[16,128]{1,0:T(8,128)S(1)}, f32[16,128]{1,0:T(8,128)S(1)}, u32[]{:S(2)}, u32[]{:S(2)}) %collective-permute-start.11) | collective-permute-done | bytes 8224 | tf_op jit(solution)/shard_map/ppermute | solution.py:92
  26.7 0.5 collective-permute-start.6
  27.8 1.5 %collective-permute-start = (f32[16,128]{1,0:T(8,128)S(1)}, f32[16,128]{1,0:T(8,128)S(1)}, u32[]{:S(2)}, u32[]{:S(2)}) collective-permute-start(f32[16,128]{1,0:T(8,128)S(1)} %pad_maximum_fusion.refs_0_), channel_id=1, source_target_pairs={{0,8},{4,12},{8,0},{12,4},{1,9},{5,13},{9,1},{13,5},{2,10},{6,14},... | collective-permute-start | bytes 24584 | tf_op jit(solution)/shard_map/ppermute | solution.py:92
  29.4 2.8 %collective-permute-done.6.refs_8_ = bf16[128,512]{1,0:T(8,128)(2,1)S(1)} collective-permute-done((bf16[128,512]{1,0:T(8,128)(2,1)S(1)}, bf16[128,512]{1,0:T(8,128)(2,1)S(1)}, u32[]{:S(2)}, u32[]{:S(2)}) %collective-permute-start.6) | collective-permute-done | bytes 131104 | tf_op jit(solution)/shard_map/ppermute | solution.py:92
  32.7 1.9 %copy-done = bf16[1,2048,768]{2,1,0:T(8,128)(2,1)S(1)} copy-done((bf16[1,2048,768]{2,1,0:T(8,128)(2,1)S(1)}, bf16[1,2048,768]{2,1,0:T(8,128)(2,1)}, u32[]{:S(2)}) %copy-start) | copy-done | bytes 3145752
  34.6 1.9 %copy-done.2 = bf16[1,2048,768]{2,1,0:T(8,128)(2,1)S(1)} copy-done((bf16[1,2048,768]{2,1,0:T(8,128)(2,1)S(1)}, bf16[1,2048,768]{2,1,0:T(8,128)(2,1)}, u32[]{:S(2)}) %copy-start.2) | copy-done | bytes 3145752
  36.5 1.9 %copy-done.3 = bf16[1,768,2048]{2,1,0:T(8,128)(2,1)S(1)} copy-done((bf16[1,768,2048]{2,1,0:T(8,128)(2,1)S(1)}, bf16[1,768,2048]{2,1,0:T(8,128)(2,1)}, u32[]{:S(2)}) %copy-start.3) | copy-done | bytes 3145752
  38.4 3.3 %expert.3 = (f32[256,1024]{1,0:T(8,128)S(1)}, bf16[256,1024]{1,0:T(8,128)(2,1)S(1)}) custom-call(s32[2]{0:T(128)S(1)} %pad_add_fusion.place, f32[16,128]{1,0:T(8,128)S(1)} %collective-permute-done.10.refs_0_, f32[16,128]{1,0:T(8,128)S(1)} %collective-permute-done.11.refs_1_, bf16[128,512]{1,0:T(8,128)(2,1)S(1)} %collective-permute-done.12.refs_2_, ...), custom_call_target="tpu_custom_call" | custom-call | flops 2415919104 | bytes 1048576 | tf_op jit(solution)/shard_map/expert/pallas_call | solution.py:137
  42.3 3.3 %expert.2 = (f32[256,1024]{1,0:T(8,128)S(1)}, bf16[256,1024]{1,0:T(8,128)(2,1)S(1)}) custom-call(s32[2]{0:T(128)S(1)} %pad_add_fusion.place, f32[16,128]{1,0:T(8,128)S(1)} %pad_maximum_fusion.refs_0_, f32[16,128]{1,0:T(8,128)S(1)} %collective-permute-done.refs_1_, bf16[128,512]{1,0:T(8,128)(2,1)S(1)} %copy-done.4, ...), custom_call_target="tpu_custom_call" | custom-call | flops 2415919104 | bytes 1048576 | tf_op jit(solution)/shard_map/expert/pallas_call | solution.py:137
  45.8 0.6 collective-permute-start.25
  46.4 1.5 %collective-permute-start.21 = (bf16[128,512]{1,0:T(8,128)(2,1)S(1)}, bf16[128,512]{1,0:T(8,128)(2,1)S(1)}, u32[]{:S(2)}, u32[]{:S(2)}) collective-permute-start(bf16[128,512]{1,0:T(8,128)(2,1)S(1)} %get-tuple-element.24), channel_id=1, source_target_pairs={{0,2},{1,3},{2,0},{3,1},{4,6},{5,7},{6,4},{7,5},{8,10},{9,11},{10,... | collective-permute-start | bytes 393224 | tf_op jit(solution)/shard_map/ppermute | solution.py:92
  48.0 0.6 collective-permute-start.23
  48.6 1.5 %collective-permute-start.9 = (bf16[128,512]{1,0:T(8,128)(2,1)S(1)}, bf16[128,512]{1,0:T(8,128)(2,1)S(1)}, u32[]{:S(2)}, u32[]{:S(2)}) collective-permute-start(bf16[128,512]{1,0:T(8,128)(2,1)S(1)} %get-tuple-element.20), channel_id=1, source_target_pairs={{0,2},{1,3},{2,0},{3,1},{4,6},{5,7},{6,4},{7,5},{8,10},{9,11},{10,... | collective-permute-start | bytes 393224 | tf_op jit(solution)/shard_map/ppermute | solution.py:92
  50.1 2.1 %collective-permute-done.25.refs_1_ = bf16[128,512]{1,0:T(8,128)(2,1)S(1)} collective-permute-done((bf16[128,512]{1,0:T(8,128)(2,1)S(1)}, bf16[128,512]{1,0:T(8,128)(2,1)S(1)}, u32[]{:S(2)}, u32[]{:S(2)}) %collective-permute-start.25) | collective-permute-done | bytes 131104 | tf_op jit(solution)/shard_map/ppermute | solution.py:92
  52.3 2.8 %collective-permute-start.26 = (bf16[128,512]{1,0:T(8,128)(2,1)S(1)}, bf16[128,512]{1,0:T(8,128)(2,1)S(1)}, u32[]{:S(2)}, u32[]{:S(2)}) collective-permute-start(bf16[128,512]{1,0:T(8,128)(2,1)S(1)} %total.6), channel_id=1, source_target_pairs={{0,12},{4,8},{8,4},{12,0},{1,13},{5,9},{9,5},{13,1},{2,14},{6,10},... | collective-permute-start | bytes 393224 | tf_op jit(solution)/shard_map/ppermute | solution.py:92
  55.4 2.5 %collective-permute-done.23.refs_1_ = bf16[128,512]{1,0:T(8,128)(2,1)S(1)} collective-permute-done((bf16[128,512]{1,0:T(8,128)(2,1)S(1)}, bf16[128,512]{1,0:T(8,128)(2,1)S(1)}, u32[]{:S(2)}, u32[]{:S(2)}) %collective-permute-start.23) | collective-permute-done | bytes 131104 | tf_op jit(solution)/shard_map/ppermute | solution.py:92
  57.9 1.6 %collective-permute-start.24 = (bf16[128,512]{1,0:T(8,128)(2,1)S(1)}, bf16[128,512]{1,0:T(8,128)(2,1)S(1)}, u32[]{:S(2)}, u32[]{:S(2)}) collective-permute-start(bf16[128,512]{1,0:T(8,128)(2,1)S(1)} %total.5), channel_id=1, source_target_pairs={{0,8},{4,12},{8,0},{12,4},{1,9},{5,13},{9,1},{13,5},{2,10},{6,14},... | collective-permute-start | bytes 393224 | tf_op jit(solution)/shard_map/ppermute | solution.py:92
  59.5 0.7 collective-permute-done.9.refs_1_
  60.4 2.2 %collective-permute-done.22.refs_2_ = bf16[128,512]{1,0:T(8,128)(2,1)S(1)} collective-permute-done((bf16[128,512]{1,0:T(8,128)(2,1)S(1)}, bf16[128,512]{1,0:T(8,128)(2,1)S(1)}, u32[]{:S(2)}, u32[]{:S(2)}) %collective-permute-start.22) | collective-permute-done | bytes 131104 | tf_op jit(solution)/shard_map/ppermute | solution.py:92
  62.6 3.5 %collective-permute-done.24.refs_3_ = bf16[128,512]{1,0:T(8,128)(2,1)S(1)} collective-permute-done((bf16[128,512]{1,0:T(8,128)(2,1)S(1)}, bf16[128,512]{1,0:T(8,128)(2,1)S(1)}, u32[]{:S(2)}, u32[]{:S(2)}) %collective-permute-start.24) | collective-permute-done | bytes 131104 | tf_op jit(solution)/shard_map/ppermute | solution.py:92
  66.1 0.7 %total.7 = bf16[128,512]{1,0:T(8,128)(2,1)} custom-call(f32[128,512]{1,0:T(8,128)S(1)} %get-tuple-element.19.refs_0_, bf16[128,512]{1,0:T(8,128)(2,1)S(1)} %collective-permute-done.9.refs_1_, bf16[128,512]{1,0:T(8,128)(2,1)S(1)} %collective-permute-done.22.refs_2_, bf16[128,512]{1,0:T(8,128)(2,1)S(1)} %collective-permute-done.24.refs_3_, ...), custom_call_target="tpu_custom_call" | custom-call | flops 327680 | bytes 65536 | tf_op jit(solution)/shard_map/total/pallas_call | solution.py:189
  (43 shorter events, 3.2 us)
Async XLA Ops:
  0.0 7.1 %collective-permute-start.12 = (bf16[128,512]{1,0:T(8,128)(2,1)}, bf16[128,512]{1,0:T(8,128)(2,1)S(1)}, u32[]{:S(2)}, u32[]{:S(2)}) collective-permute-start(bf16[128,512]{1,0:T(8,128)(2,1)} %refs_2_.1), channel_id=1, source_target_pairs={{0,4},{4,0},{8,12},{12,8},{1,5},{5,1},{9,13},{13,9},{2,6},{6,2},{1... | collective-permute-start | bytes 393224 | tf_op jit(solution)/shard_map/ppermute | solution.py:92
  3.1 9.9 %collective-permute-start.16 = (bf16[128,512]{1,0:T(8,128)(2,1)}, bf16[128,512]{1,0:T(8,128)(2,1)S(1)}, u32[]{:S(2)}, u32[]{:S(2)}) collective-permute-start(bf16[128,512]{1,0:T(8,128)(2,1)} %refs_2_.1), channel_id=1, source_target_pairs={{0,12},{4,8},{8,4},{12,0},{1,13},{5,9},{9,5},{13,1},{2,14},{6,10},... | collective-permute-start | bytes 393224 | tf_op jit(solution)/shard_map/ppermute | solution.py:92
  5.5 20.6 %collective-permute-start.4 = (bf16[128,512]{1,0:T(8,128)(2,1)}, bf16[128,512]{1,0:T(8,128)(2,1)S(1)}, u32[]{:S(2)}, u32[]{:S(2)}) collective-permute-start(bf16[128,512]{1,0:T(8,128)(2,1)} %refs_2_.1), channel_id=1, source_target_pairs={{0,8},{4,12},{8,0},{12,4},{1,9},{5,13},{9,1},{13,5},{2,10},{6,14},... | collective-permute-start | bytes 393224 | tf_op jit(solution)/shard_map/ppermute | solution.py:92
  5.6 21.0 %collective-permute-start.2 = (bf16[128,512]{1,0:T(8,128)(2,1)}, bf16[128,512]{1,0:T(8,128)(2,1)S(1)}, u32[]{:S(2)}, u32[]{:S(2)}) collective-permute-start(bf16[128,512]{1,0:T(8,128)(2,1)} %refs_2_.1), channel_id=1, source_target_pairs={{0,2},{1,3},{2,0},{3,1},{4,6},{5,7},{6,4},{7,5},{8,10},{9,11},{10,... | collective-permute-start | bytes 393224 | tf_op jit(solution)/shard_map/ppermute | solution.py:92
  7.1 20.1 %collective-permute-start.14 = (bf16[128,512]{1,0:T(8,128)(2,1)S(1)}, bf16[128,512]{1,0:T(8,128)(2,1)S(1)}, u32[]{:S(2)}, u32[]{:S(2)}) collective-permute-start(bf16[128,512]{1,0:T(8,128)(2,1)S(1)} %collective-permute-done.12.refs_2_), channel_id=1, source_target_pairs={{0,2},{1,3},{2,0},{3,1},{4,6},{5,7},{6,4},{7,5},{8,10},{9,11},{10,... | collective-permute-start | bytes 393224 | tf_op jit(solution)/shard_map/ppermute | solution.py:92
  13.0 14.2 %collective-permute-start.18 = (bf16[128,512]{1,0:T(8,128)(2,1)S(1)}, bf16[128,512]{1,0:T(8,128)(2,1)S(1)}, u32[]{:S(2)}, u32[]{:S(2)}) collective-permute-start(bf16[128,512]{1,0:T(8,128)(2,1)S(1)} %collective-permute-done.16.refs_6_), channel_id=1, source_target_pairs={{0,2},{1,3},{2,0},{3,1},{4,6},{5,7},{6,4},{7,5},{8,10},{9,11},{10,... | collective-permute-start | bytes 393224 | tf_op jit(solution)/shard_map/ppermute | solution.py:92
  15.9 4.9 %collective-permute-start.10 = (f32[16,128]{1,0:T(8,128)S(1)}, f32[16,128]{1,0:T(8,128)S(1)}, u32[]{:S(2)}, u32[]{:S(2)}) collective-permute-start(f32[16,128]{1,0:T(8,128)S(1)} %pad_maximum_fusion.refs_0_), channel_id=1, source_target_pairs={{0,4},{4,0},{8,12},{12,8},{1,5},{5,1},{9,13},{13,9},{2,6},{6,2},{1... | collective-permute-start | bytes 24584 | tf_op jit(solution)/shard_map/ppermute | solution.py:92
  20.7 5.4 %collective-permute-start.11 = (f32[16,128]{1,0:T(8,128)S(1)}, f32[16,128]{1,0:T(8,128)S(1)}, u32[]{:S(2)}, u32[]{:S(2)}) collective-permute-start(f32[16,128]{1,0:T(8,128)S(1)} %pad_maximum_fusion.refs_0_), channel_id=1, source_target_pairs={{0,12},{4,8},{8,4},{12,0},{1,13},{5,9},{9,5},{13,1},{2,14},{6,10},... | collective-permute-start | bytes 24584 | tf_op jit(solution)/shard_map/ppermute | solution.py:92
  26.2 1.6 %collective-permute-start.13 = (bf16[128,512]{1,0:T(8,128)(2,1)S(1)}, bf16[128,512]{1,0:T(8,128)(2,1)S(1)}, u32[]{:S(2)}, u32[]{:S(2)}) collective-permute-start(bf16[128,512]{1,0:T(8,128)(2,1)S(1)} %collective-permute-done.12.refs_2_), channel_id=1, source_target_pairs={{0,1},{1,0},{2,3},{3,2},{4,5},{5,4},{6,7},{7,6},{8,9},{9,8},{10,11... | collective-permute-start | bytes 393224 | tf_op jit(solution)/shard_map/ppermute | solution.py:92
  26.2 3.2 %collective-permute-start.17 = (bf16[128,512]{1,0:T(8,128)(2,1)S(1)}, bf16[128,512]{1,0:T(8,128)(2,1)S(1)}, u32[]{:S(2)}, u32[]{:S(2)}) collective-permute-start(bf16[128,512]{1,0:T(8,128)(2,1)S(1)} %collective-permute-done.16.refs_6_), channel_id=1, source_target_pairs={{0,1},{1,0},{2,3},{3,2},{4,5},{5,4},{6,7},{7,6},{8,9},{9,8},{10,11... | collective-permute-start | bytes 393224 | tf_op jit(solution)/shard_map/ppermute | solution.py:92
  26.7 5.5 %collective-permute-start.6 = (bf16[128,512]{1,0:T(8,128)(2,1)S(1)}, bf16[128,512]{1,0:T(8,128)(2,1)S(1)}, u32[]{:S(2)}, u32[]{:S(2)}) collective-permute-start(bf16[128,512]{1,0:T(8,128)(2,1)S(1)} %collective-permute-done.4.refs_6_), channel_id=1, source_target_pairs={{0,2},{1,3},{2,0},{3,1},{4,6},{5,7},{6,4},{7,5},{8,10},{9,11},{10,... | collective-permute-start | bytes 393224 | tf_op jit(solution)/shard_map/ppermute | solution.py:92
  27.2 4.9 %collective-permute-start.15 = (bf16[128,512]{1,0:T(8,128)(2,1)S(1)}, bf16[128,512]{1,0:T(8,128)(2,1)S(1)}, u32[]{:S(2)}, u32[]{:S(2)}) collective-permute-start(bf16[128,512]{1,0:T(8,128)(2,1)S(1)} %collective-permute-done.14.refs_4_), channel_id=1, source_target_pairs={{0,1},{1,0},{2,3},{3,2},{4,5},{5,4},{6,7},{7,6},{8,9},{9,8},{10,11... | collective-permute-start | bytes 393224 | tf_op jit(solution)/shard_map/ppermute | solution.py:92
  27.2 5.4 %collective-permute-start.19 = (bf16[128,512]{1,0:T(8,128)(2,1)S(1)}, bf16[128,512]{1,0:T(8,128)(2,1)S(1)}, u32[]{:S(2)}, u32[]{:S(2)}) collective-permute-start(bf16[128,512]{1,0:T(8,128)(2,1)S(1)} %collective-permute-done.18.refs_8_), channel_id=1, source_target_pairs={{0,1},{1,0},{2,3},{3,2},{4,5},{5,4},{6,7},{7,6},{8,9},{9,8},{10,11... | collective-permute-start | bytes 393224 | tf_op jit(solution)/shard_map/ppermute | solution.py:92
  27.8 13.9 %collective-permute-start = (f32[16,128]{1,0:T(8,128)S(1)}, f32[16,128]{1,0:T(8,128)S(1)}, u32[]{:S(2)}, u32[]{:S(2)}) collective-permute-start(f32[16,128]{1,0:T(8,128)S(1)} %pad_maximum_fusion.refs_0_), channel_id=1, source_target_pairs={{0,8},{4,12},{8,0},{12,4},{1,9},{5,13},{9,1},{13,5},{2,10},{6,14},... | collective-permute-start | bytes 24584 | tf_op jit(solution)/shard_map/ppermute | solution.py:92
  29.4 12.9 %collective-permute-start.1 = (bf16[128,512]{1,0:T(8,128)(2,1)}, bf16[128,512]{1,0:T(8,128)(2,1)S(1)}, u32[]{:S(2)}, u32[]{:S(2)}) collective-permute-start(bf16[128,512]{1,0:T(8,128)(2,1)} %refs_2_.1), channel_id=1, source_target_pairs={{0,1},{1,0},{2,3},{3,2},{4,5},{5,4},{6,7},{7,6},{8,9},{9,8},{10,11... | collective-permute-start | bytes 393224 | tf_op jit(solution)/shard_map/ppermute | solution.py:92
  32.2 10.1 %collective-permute-start.5 = (bf16[128,512]{1,0:T(8,128)(2,1)S(1)}, bf16[128,512]{1,0:T(8,128)(2,1)S(1)}, u32[]{:S(2)}, u32[]{:S(2)}) collective-permute-start(bf16[128,512]{1,0:T(8,128)(2,1)S(1)} %collective-permute-done.4.refs_6_), channel_id=1, source_target_pairs={{0,1},{1,0},{2,3},{3,2},{4,5},{5,4},{6,7},{7,6},{8,9},{9,8},{10,11... | collective-permute-start | bytes 393224 | tf_op jit(solution)/shard_map/ppermute | solution.py:92
  32.2 10.1 %collective-permute-start.3 = (bf16[128,512]{1,0:T(8,128)(2,1)S(1)}, bf16[128,512]{1,0:T(8,128)(2,1)S(1)}, u32[]{:S(2)}, u32[]{:S(2)}) collective-permute-start(bf16[128,512]{1,0:T(8,128)(2,1)S(1)} %collective-permute-done.2.refs_4_), channel_id=1, source_target_pairs={{0,1},{1,0},{2,3},{3,2},{4,5},{5,4},{6,7},{7,6},{8,9},{9,8},{10,11... | collective-permute-start | bytes 393224 | tf_op jit(solution)/shard_map/ppermute | solution.py:92
  32.7 9.6 %collective-permute-start.7 = (bf16[128,512]{1,0:T(8,128)(2,1)S(1)}, bf16[128,512]{1,0:T(8,128)(2,1)S(1)}, u32[]{:S(2)}, u32[]{:S(2)}) collective-permute-start(bf16[128,512]{1,0:T(8,128)(2,1)S(1)} %collective-permute-done.6.refs_8_), channel_id=1, source_target_pairs={{0,1},{1,0},{2,3},{3,2},{4,5},{5,4},{6,7},{7,6},{8,9},{9,8},{10,11... | collective-permute-start | bytes 393224 | tf_op jit(solution)/shard_map/ppermute | solution.py:92
  32.7 1.9 %copy-start = (bf16[1,2048,768]{2,1,0:T(8,128)(2,1)S(1)}, bf16[1,2048,768]{2,1,0:T(8,128)(2,1)}, u32[]{:S(2)}) copy-start(bf16[1,2048,768]{2,1,0:T(8,128)(2,1)} %param.9) | copy-start | bytes 9437188
  34.6 1.9 %copy-start.2 = (bf16[1,2048,768]{2,1,0:T(8,128)(2,1)S(1)}, bf16[1,2048,768]{2,1,0:T(8,128)(2,1)}, u32[]{:S(2)}) copy-start(bf16[1,2048,768]{2,1,0:T(8,128)(2,1)} %param.10) | copy-start | bytes 9437188
  36.5 1.9 %copy-start.3 = (bf16[1,768,2048]{2,1,0:T(8,128)(2,1)S(1)}, bf16[1,768,2048]{2,1,0:T(8,128)(2,1)}, u32[]{:S(2)}) copy-start(bf16[1,768,2048]{2,1,0:T(8,128)(2,1)} %param.11) | copy-start | bytes 9437188
  38.4 3.8 %copy-start.1 = (bf16[1,2048,768]{2,1,0:T(8,128)(2,1)S(1)}, bf16[1,2048,768]{2,1,0:T(8,128)(2,1)}, u32[]{:S(2)}) copy-start(bf16[1,2048,768]{2,1,0:T(8,128)(2,1)} %param.9) | copy-start | bytes 9437188
  38.4 3.8 %copy-start.4 = (bf16[128,512]{1,0:T(8,128)(2,1)S(1)}, bf16[128,512]{1,0:T(8,128)(2,1)}, u32[]{:S(2)}) copy-start(bf16[128,512]{1,0:T(8,128)(2,1)} %refs_2_.1) | copy-start | bytes 393220
  41.7 4.0 %collective-permute-start.20 = (bf16[256,1024]{1,0:T(8,128)(2,1)S(1)}, bf16[256,1024]{1,0:T(8,128)(2,1)S(1)}, u32[]{:S(2)}, u32[]{:S(2)}) collective-permute-start(bf16[256,1024]{1,0:T(8,128)(2,1)S(1)} %get-tuple-element.22), channel_id=1, source_target_pairs={{0,1},{1,0},{2,3},{3,2},{4,5},{5,4},{6,7},{7,6},{8,9},{9,8},{10,11... | collective-permute-start | bytes 1572872 | tf_op jit(solution)/shard_map/ppermute | solution.py:92
  45.6 2.3 %collective-permute-start.8 = (bf16[256,1024]{1,0:T(8,128)(2,1)S(1)}, bf16[256,1024]{1,0:T(8,128)(2,1)S(1)}, u32[]{:S(2)}, u32[]{:S(2)}) collective-permute-start(bf16[256,1024]{1,0:T(8,128)(2,1)S(1)} %get-tuple-element.18), channel_id=1, source_target_pairs={{0,1},{1,0},{2,3},{3,2},{4,5},{5,4},{6,7},{7,6},{8,9},{9,8},{10,11... | collective-permute-start | bytes 1572872 | tf_op jit(solution)/shard_map/ppermute | solution.py:92
  45.8 6.4 %collective-permute-start.25 = (bf16[128,512]{1,0:T(8,128)(2,1)S(1)}, bf16[128,512]{1,0:T(8,128)(2,1)S(1)}, u32[]{:S(2)}, u32[]{:S(2)}) collective-permute-start(bf16[128,512]{1,0:T(8,128)(2,1)S(1)} %get-tuple-element.28), channel_id=1, source_target_pairs={{0,2},{1,3},{2,0},{3,1},{4,6},{5,7},{6,4},{7,5},{8,10},{9,11},{10,... | collective-permute-start | bytes 393224 | tf_op jit(solution)/shard_map/ppermute | solution.py:92
  46.4 8.7 %collective-permute-start.21 = (bf16[128,512]{1,0:T(8,128)(2,1)S(1)}, bf16[128,512]{1,0:T(8,128)(2,1)S(1)}, u32[]{:S(2)}, u32[]{:S(2)}) collective-permute-start(bf16[128,512]{1,0:T(8,128)(2,1)S(1)} %get-tuple-element.24), channel_id=1, source_target_pairs={{0,2},{1,3},{2,0},{3,1},{4,6},{5,7},{6,4},{7,5},{8,10},{9,11},{10,... | collective-permute-start | bytes 393224 | tf_op jit(solution)/shard_map/ppermute | solution.py:92
  48.0 9.8 %collective-permute-start.23 = (bf16[128,512]{1,0:T(8,128)(2,1)S(1)}, bf16[128,512]{1,0:T(8,128)(2,1)S(1)}, u32[]{:S(2)}, u32[]{:S(2)}) collective-permute-start(bf16[128,512]{1,0:T(8,128)(2,1)S(1)} %get-tuple-element.26), channel_id=1, source_target_pairs={{0,2},{1,3},{2,0},{3,1},{4,6},{5,7},{6,4},{7,5},{8,10},{9,11},{10,... | collective-permute-start | bytes 393224 | tf_op jit(solution)/shard_map/ppermute | solution.py:92
  48.6 11.5 %collective-permute-start.9 = (bf16[128,512]{1,0:T(8,128)(2,1)S(1)}, bf16[128,512]{1,0:T(8,128)(2,1)S(1)}, u32[]{:S(2)}, u32[]{:S(2)}) collective-permute-start(bf16[128,512]{1,0:T(8,128)(2,1)S(1)} %get-tuple-element.20), channel_id=1, source_target_pairs={{0,2},{1,3},{2,0},{3,1},{4,6},{5,7},{6,4},{7,5},{8,10},{9,11},{10,... | collective-permute-start | bytes 393224 | tf_op jit(solution)/shard_map/ppermute | solution.py:92
  52.3 8.1 %collective-permute-start.26 = (bf16[128,512]{1,0:T(8,128)(2,1)S(1)}, bf16[128,512]{1,0:T(8,128)(2,1)S(1)}, u32[]{:S(2)}, u32[]{:S(2)}) collective-permute-start(bf16[128,512]{1,0:T(8,128)(2,1)S(1)} %total.6), channel_id=1, source_target_pairs={{0,12},{4,8},{8,4},{12,0},{1,13},{5,9},{9,5},{13,1},{2,14},{6,10},... | collective-permute-start | bytes 393224 | tf_op jit(solution)/shard_map/ppermute | solution.py:92
  55.1 7.5 %collective-permute-start.22 = (bf16[128,512]{1,0:T(8,128)(2,1)S(1)}, bf16[128,512]{1,0:T(8,128)(2,1)S(1)}, u32[]{:S(2)}, u32[]{:S(2)}) collective-permute-start(bf16[128,512]{1,0:T(8,128)(2,1)S(1)} %total.4), channel_id=1, source_target_pairs={{0,4},{4,0},{8,12},{12,8},{1,5},{5,1},{9,13},{13,9},{2,6},{6,2},{1... | collective-permute-start | bytes 393224 | tf_op jit(solution)/shard_map/ppermute | solution.py:92
  57.9 8.2 %collective-permute-start.24 = (bf16[128,512]{1,0:T(8,128)(2,1)S(1)}, bf16[128,512]{1,0:T(8,128)(2,1)S(1)}, u32[]{:S(2)}, u32[]{:S(2)}) collective-permute-start(bf16[128,512]{1,0:T(8,128)(2,1)S(1)} %total.5), channel_id=1, source_target_pairs={{0,8},{4,12},{8,0},{12,4},{1,9},{5,13},{9,1},{13,5},{2,10},{6,14},... | collective-permute-start | bytes 393224 | tf_op jit(solution)/shard_map/ppermute | solution.py:92
